TPU v7x, 256 devices: a whole 4x4x8 slice. The times are simulated.
256 devices in a mesh: row: 16 (over z, y_lo), col: 8 (over x, y_hi), rep: 2 (over core).
Axes of the slice: x: 4, y: 4 (y_hi: 2, y_lo: 2; y = y_hi * 2 + y_lo), z: 8, core: 2. Of those that a mesh axis runs over, the one named last changes fastest.
Arguments:
- activations: bfloat16 [2048, 7168], P(('col', 'rep'), 'row'), may hold values from -6 to 6
- out_grad: bfloat16 [2048, 7168], P(('col', 'rep'), 'row'), may hold values from -1.5 to 1.5
- up_codes: int32 [7168, 18432], P('row', 'col'), may hold values from 0 to 253
- up_scales: int32 [224, 18432], P('row', 'col'), may hold values from -15 to -12
- down_codes: int32 [18432, 7168], P('col', 'row'), may hold values from 0 to 253
- down_scales: int32 [576, 7168], P('col', 'row'), may hold values from -15 to -12
Outputs:
- layer_out: bfloat16 [2048, 7168], P(('col', 'rep'), 'row')
- in_grad: bfloat16 [2048, 7168], P(('col', 'rep'), 'row')
- up_grad: bfloat16 [7168, 18432], P('row', 'col')
- down_grad: bfloat16 [18432, 7168], P('col', 'row')
All inputs are finite; a program needn't handle non-finite values.
Results may differ from a plain program's by a relative error of at most 0.025.
Values may be sent and summed in bfloat16 or wider, within the bound.
A program may use at most 128 MiB of HBM per device.

v0:
```python
import jax
import jax.numpy as jnp
from jax import lax
from jax.sharding import PartitionSpec as P

BLOCK = 32


def decode(code_words, scale_exps, block_size):
    sign_bit = code_words // 127
    magnitude = code_words % 127
    exponent = magnitude // 8
    mantissa = magnitude % 8
    normal = exponent > 0
    rows_count = scale_exps.shape[0]
    cols_count = scale_exps.shape[1]
    scale_grid = jnp.broadcast_to(
        scale_exps[:, None, :], (rows_count, block_size, cols_count)
    ).reshape(code_words.shape)
    shift_count = -(jnp.where(normal, exponent - 10, -9) + scale_grid)
    factor = jnp.ones(code_words.shape, jnp.float32)
    halvings = (0.5, 0.25, 0.0625, 0.00390625, 1.52587890625e-05)
    for position in range(5):
        chosen = shift_count // 2**position % 2 == 1
        factor = factor * jnp.where(chosen, jnp.float32(halvings[position]), jnp.float32(1.0))
    mant_value = jnp.where(normal, mantissa + 8, mantissa).astype(jnp.float32)
    signed = (1 - 2 * sign_bit).astype(jnp.float32)
    return (mant_value * factor * signed).astype(jnp.bfloat16)


def gelu_parts(pre_total):
    cdf_value = 0.5 * (1.0 + jax.scipy.special.erf(pre_total * 0.7071067811865476))
    density = jnp.exp(-0.5 * pre_total * pre_total) * 0.3989422804014327
    return (pre_total * cdf_value, cdf_value + pre_total * density)


def replica_total(partial_value):
    return lax.psum(partial_value.astype(jnp.bfloat16), "rep")


def body(activations, out_grad, up_codes, up_scales, down_codes, down_scales):
    contract_last = (((1,), (1,)), ((), ()))
    contract_first = (((0,), (0,)), ((), ()))
    up_weight = decode(up_codes, up_scales, BLOCK)
    down_weight = decode(down_codes, down_scales, BLOCK)
    acts_all, grads_all = (
        lax.all_gather(activations, "col", axis=0, tiled=True),
        lax.all_gather(out_grad, "col", axis=0, tiled=True),
    )
    pre_part = jnp.dot(acts_all, up_weight, preferred_element_type=jnp.float32)
    back_part = lax.dot_general(
        grads_all, down_weight, contract_last, preferred_element_type=jnp.float32
    )
    pre_total, back_total = (
        lax.psum(pre_part.astype(jnp.bfloat16), "row").astype(jnp.float32),
        lax.psum(back_part.astype(jnp.bfloat16), "row").astype(jnp.float32),
    )
    activated, gelu_slope = gelu_parts(pre_total)
    gelu_out = activated.astype(jnp.bfloat16)
    hidden_grad = (back_total * gelu_slope).astype(jnp.bfloat16)
    down_grad = replica_total(
        lax.dot_general(gelu_out, grads_all, contract_first, preferred_element_type=jnp.float32)
    )
    out_part = jnp.dot(gelu_out, down_weight, preferred_element_type=jnp.float32)
    in_part = lax.dot_general(
        hidden_grad, up_weight, contract_last, preferred_element_type=jnp.float32
    )
    out_sum, in_sum = (
        lax.psum_scatter(
            out_part.astype(jnp.bfloat16), "col", scatter_dimension=0, tiled=True
        ).astype(jnp.float32),
        lax.psum_scatter(
            in_part.astype(jnp.bfloat16), "col", scatter_dimension=0, tiled=True
        ).astype(jnp.float32),
    )
    layer_out = out_sum.astype(jnp.bfloat16)
    in_grad = in_sum.astype(jnp.bfloat16)
    up_grad = replica_total(
        lax.dot_general(acts_all, hidden_grad, contract_first, preferred_element_type=jnp.float32)
    )
    return (layer_out, in_grad, up_grad, down_grad)


def solution(mesh):
    placed = (
        P(("col", "rep"), "row"),
        P(("col", "rep"), "row"),
        P("row", "col"),
        P("row", "col"),
        P("col", "row"),
        P("col", "row"),
    )
    return jax.shard_map(
        body,
        mesh=mesh,
        in_specs=placed,
        out_specs=(
            P(("col", "rep"), "row"),
            P(("col", "rep"), "row"),
            P("row", "col"),
            P("col", "row"),
        ),
        check_vma=False,
    )
```

profile of v0, /device:TPU:1, one launch (start us, length us, event | category | flops | bytes accessed | tf_op | source)
XLA Modules:
  0.0 786.9 jit_solution(16063781059810175605)
XLA Ops:
  7.2 0.0 all-reduce.5.cloned.1.call-start
  7.2 31.7 %all_gather.6 = bf16[1024,448]{0,1:T(8,128)(2,1)S(1)} all-gather(bf16[128,448]{0,1:T(8,128)(2,1)} %param.6), channel_id=1, replica_groups=mesh['row'=16,'col'=8,'rep'=2] {'col'}, dimensions={0}, use_global_device_ids=true | all-gather | bytes 1032192 | tf_op jit(solution)/shard_map/all_gather | solution.py:47
  38.9 0.0 copy-start.6
  38.9 28.3 %all_gather.7 = bf16[1024,448]{0,1:T(8,128)(2,1)S(1)} all-gather(bf16[128,448]{0,1:T(8,128)(2,1)} %param.7), channel_id=1, replica_groups=mesh['row'=16,'col'=8,'rep'=2] {'col'}, dimensions={0}, use_global_device_ids=true | all-gather | bytes 1032192 | tf_op jit(solution)/shard_map/all_gather | solution.py:48
  67.2 0.0 copy-start.1
  67.2 0.0 copy-start.7
  67.2 6.2 copy.14
  73.4 0.0 copy-done.7
  73.4 26.8 %fusion.42 = bf16[448,2304]{1,0:T(8,128)(2,1)S(1)} fusion(s32[448,2304]{1,0:T(8,128)} %param.8, s32[14,2304]{1,0:T(8,128)S(1)} %copy-done.7), kind=kLoop, calls=%fused_computation.127 | loop fusion | flops 155860992 | bytes 6322176 | tf_op jit(solution)/shard_map/convert_element_type | solution.py:28
  100.3 0.0 copy-done.6
  100.3 0.0 copy-start.3
  100.3 0.0 slice-start.1
  100.3 0.0 copy-start.8
  100.3 4.3 fusion.9
  104.6 0.0 copy-done.3
  104.6 0.0 slice-done
  104.6 0.0 slice-done.1
  104.6 0.0 copy-done.8
  104.6 29.5 %fusion.15 = bf16[2304,448]{1,0:T(8,128)(2,1)S(1)} fusion(s32[2304,448]{1,0:T(8,128)S(1)} %bitcast.27, s32[72,448]{1,0:T(8,128)S(1)} %copy-done.8), kind=kLoop, calls=%fused_computation.94 | loop fusion | flops 155860992 | bytes 6322176 | tf_op jit(solution)/shard_map/convert_element_type | solution.py:28
  134.1 0.0 copy-done.1
  134.1 4.3 fusion.10
  138.4 0.0 all-reduce.5.cloned.1.call-update
  138.4 0.0 reduce-scatter.9.cloned.1.call-start
  138.5 419.3 %all-reduce.5.cloned.1.call-done = (bf16[1024,2304]{0,1:T(8,128)(2,1)}, bf16[1024,2304]{0,1:T(8,128)(2,1)}) async-done(((bf16[1024,2304]{0,1:T(8,128)(2,1)}, bf16[1024,2304]{0,1:T(8,128)(2,1)}), (bf16[1024,2304]{0,1:T(8,128)(2,1)}, bf16[1024,2304]{0,1:T(8,128)(2,1)})) %all-reduce.5.cloned.1.call-update) | async-done | bytes 9437200 | tf_op jit(solution)/shard_map/psum | solution.py:55
  557.8 11.3 %fusion.8 = (bf16[1024,2304]{0,1:T(8,128)(2,1)S(1)}, f32[1024,2304]{0,1:T(8,128)}) fusion(bf16[1024,2304]{0,1:T(8,128)(2,1)} %get-tuple-element.4, bf16[1024,2304]{0,1:T(8,128)(2,1)} %get-tuple-element.5), kind=kLoop, calls=%fused_computation.13 | loop fusion | flops 28311552 | bytes 23592960 | tf_op jit(solution)/shard_map/convert_element_type | solution.py:60
  569.1 2.1 copy-done
  571.3 0.0 copy-done.4
  571.3 2.3 convolution_convert_fusion.4
  573.6 1.3 copy.19
  574.9 0.0 reduce-scatter.9.cloned.1.call-update
  574.9 0.2 reduce-scatter.7.cloned.1.call-start
  575.1 7.4 convolution_convert_fusion.5
  582.5 1.3 copy.17
  583.8 0.0 reduce-scatter.7.cloned.1.call-update
  583.8 0.0 copy-start.2
  583.8 0.0 all-reduce.7.cloned.1.call-start
  583.9 6.3 fusion.65
  590.2 0.0 copy-done.2
  590.2 8.7 %convolution_convert_fusion.2 = bf16[2304,448]{0,1:T(8,128)(2,1)} fusion(bf16[1024,448]{0,1:T(8,128)(2,1)S(1)} %copy-done.2, f32[1024,2304]{0,1:T(8,128)} %get-tuple-element.9, bf16[1024,2304]{0,1:T(8,128)(2,1)} %get-tuple-element.4), kind=kOutput, calls=%fused_computation.121 | convolution fusion | flops 2122039296 | bytes 17137664 | tf_op jit(solution)/shard_map/dot_general | solution.py:62
  598.9 0.0 all-reduce.7.cloned.1.call-update
  599.0 52.1 %reduce-scatter.9.cloned.1.call-done = bf16[128,448]{1,0:T(8,128)(2,1)} async-done(((bf16[1024,448]{1,0:T(8,128)(2,1)}), bf16[128,448]{1,0:T(8,128)(2,1)}) %reduce-scatter.9.cloned.1.call-update) | async-done | bytes 114704
  651.1 1.7 copy.20
  652.7 78.9 %reduce-scatter.7.cloned.1.call-done = bf16[128,448]{1,0:T(8,128)(2,1)} async-done(((bf16[1024,448]{1,0:T(8,128)(2,1)}), bf16[128,448]{1,0:T(8,128)(2,1)}) %reduce-scatter.7.cloned.1.call-update) | async-done | bytes 114704
  731.6 1.7 copy.18
  733.3 42.6 %all-reduce.7.cloned.1.call-done = (bf16[448,2304]{1,0:T(8,128)(2,1)}, bf16[2304,448]{0,1:T(8,128)(2,1)}) async-done(((bf16[448,2304]{1,0:T(8,128)(2,1)}, bf16[2304,448]{0,1:T(8,128)(2,1)}), (bf16[448,2304]{1,0:T(8,128)(2,1)}, bf16[2304,448]{0,1:T(8,128)(2,1)})) %all-reduce.7.cloned.1.call-update) | async-done | bytes 4128784 | tf_op jit(solution)/shard_map/psum | solution.py:38
  775.9 3.2 copy.25
  779.1 0.0 copy-done.5
  779.1 1.3 copy.26
  (5 shorter events, 0.0 us)
Async XLA Ops:
  7.2 550.6 %all-reduce.5.cloned.1.call-start = ((), (), s32[]{:S(2)}) async-start(), calls=%async_computation.4 | async-start | bytes 18874368 | tf_op jit(solution)/shard_map/psum | solution.py:55
  38.9 61.4 %copy-start.6 = (bf16[1024,448]{0,1:T(8,128)(2,1)}, bf16[1024,448]{0,1:T(8,128)(2,1)S(1)}, u32[]{:S(2)}) copy-start(bf16[1024,448]{0,1:T(8,128)(2,1)S(1)} %all_gather.6) | copy-start | bytes 2752516
  67.2 66.9 %copy-start.1 = (bf16[1024,448]{0,1:T(8,128)(2,1)}, bf16[1024,448]{0,1:T(8,128)(2,1)S(1)}, u32[]{:S(2)}) copy-start(bf16[1024,448]{0,1:T(8,128)(2,1)S(1)} %all_gather.7) | copy-start | bytes 2752516
  67.2 6.2 copy-start.7
  73.4 31.2 %slice-start = ((s8[4718592]{0:T(1024)(128)(4,1)}), s8[4194304]{0:T(1024)(128)(4,1)S(1)}, s32[]{:S(2)}) async-start(s8[4718592]{0:T(1024)(128)(4,1)} %bitcast.26), calls=%async_computation.6 | async-start | bytes 8388608
  100.3 4.3 copy-start.3
  100.3 4.3 slice-start.1
  100.3 4.3 copy-start.8
  138.4 512.6 %reduce-scatter.9.cloned.1.call-start = ((), (), s32[]{:S(2)}) async-start(), calls=%async_computation.3 | async-start | bytes 1179648
  557.8 13.4 %copy-start.4 = (bf16[448,2304]{1,0:T(8,128)(2,1)S(1)}, bf16[448,2304]{1,0:T(8,128)(2,1)}, u32[]{:S(2)}) copy-start(bf16[448,2304]{1,0:T(8,128)(2,1)} %copy-done.3) | copy-start | bytes 6193156
  569.1 2.1 copy-start
  574.9 156.8 %reduce-scatter.7.cloned.1.call-start = ((), (), s32[]{:S(2)}) async-start(), calls=%async_computation.2 | async-start | bytes 1179648
  583.8 6.4 copy-start.2
  583.8 192.0 %all-reduce.7.cloned.1.call-start = ((), (), s32[]{:S(2)}) async-start(), calls=%async_computation.5 | async-start | bytes 8257536 | tf_op jit(solution)/shard_map/psum | solution.py:38
  775.9 3.2 copy-start.5
Sparse Core Ops, SparseCore 0:
  138.6 419.2 all-reduce.4
  575.0 76.0 reduce-scatter.8
  655.5 76.0 reduce-scatter.6
  734.9 40.9 all-reduce.6
where the time goes:
time: 787 us
  waiting for transfers between devices  593 us (75%)
  other arithmetic  67.6 us (9%)
  blocking collectives  60 us (8%)
  matrix products  33.3 us (4%)
  local copies, waits for them, and re-layouts  18.8 us (2%)
  between operations  13.9 us (2%)
    psum x1, waiting for transfers between devices, body(): lax.psum(pre_part.astype(jnp.bfloat16), 'row').astype(jnp.float32)  419 us
    unnamed x6, waiting for transfers between devices  131 us
    convert_element_type x2, other arithmetic, decode(): return (mant_value * factor * signed).astype(jnp.bfloat16)  56.3 us
    psum x1, waiting for transfers between devices, replica_total(): return lax.psum(partial_value.astype(jnp.bfloat16), 'rep')  42.6 us
    all_gather x1, blocking collectives, body(): lax.all_gather(activations, 'col', axis=0, tiled=True)  31.7 us
    all_gather x1, blocking collectives, body(): lax.all_gather(out_grad, 'col', axis=0, tiled=True)  28.3 us
    unnamed x29, local copies, waits for them, and re-layouts  18.8 us
  transfers between devices with their start and end apart: 4, of which 4 were waited for; matrix products, arithmetic and copies ran while one was open for 3% of the time, Pallas kernels for 0%

commit v1 on v0

--- a/solution.py
+++ b/solution.py
@@ -44,7 +44,9 @@
     up_weight = decode(up_codes, up_scales, BLOCK)
     down_weight = decode(down_codes, down_scales, BLOCK)
     acts_all, grads_all = (
-        lax.all_gather(activations, "col", axis=0, tiled=True),
+        jnp.concatenate(
+            lax.all_to_all(jnp.stack([activations] * lax.axis_size("col")), "col", 0, 0), axis=0
+        ),
         lax.all_gather(out_grad, "col", axis=0, tiled=True),
     )
     pre_part = jnp.dot(acts_all, up_weight, preferred_element_type=jnp.float32)

time: 787 us -> 767 us (0.975)
  blocking collectives: 60 us -> 30.5 us
    all_gather x1 -> x0, blocking collectives: 31.7 us -> none  [body(): lax.all_gather(activations, 'col', axis=0, tiled=True)]
    unnamed x29 -> x27, local copies, waits for them, and re-layouts: 18.8 us -> 19.4 us
  transfers between devices with their start and end apart: 4 -> 5, of which waited for: 4 -> 4; matrix products, arithmetic and copies ran while one was open for 3% -> 12% of each run, Pallas kernels for 0% -> 0%
where the time goes in v1:
time: 767 us; the launch traced here: 766 us
  waiting for transfers between devices  589 us (77%)
  other arithmetic  68.3 us (9%)
  matrix products  35.2 us (5%)
  blocking collectives  30.5 us (4%)
  local copies, waits for them, and re-layouts  21.3 us (3%)
  between operations  13.8 us (2%)
  starting transfers between devices  7.83 us (1%)
    psum x1, waiting for transfers between devices, body(): lax.psum(pre_part.astype(jnp.bfloat16), 'row').astype(jnp.float32)  416 us
    unnamed x6, waiting for transfers between devices  131 us
    convert_element_type x2, other arithmetic, decode(): return (mant_value * factor * signed).astype(jnp.bfloat16)  57 us
    psum x1, waiting for transfers between devices, replica_total(): return lax.psum(partial_value.astype(jnp.bfloat16), 'rep')  42.6 us
    all_gather x1, blocking collectives, body(): lax.all_gather(out_grad, 'col', axis=0, tiled=True)  30.5 us
    unnamed x27, local copies, waits for them, and re-layouts  19.4 us
  transfers between devices with their start and end apart: 5, of which 4 were waited for; matrix products, arithmetic and copies ran while one was open for 12% of the time, Pallas kernels for 0%

profile of v1, /device:TPU:1, one launch (start us, length us, event | category | flops | bytes accessed | tf_op | source)
XLA Modules:
  0.0 766.5 jit_solution(2980425912790366377)
XLA Ops:
  7.2 1.9 stack.2
  9.1 7.5 all-to-all-start
  16.6 0.0 copy-start.7
  16.6 0.0 all-reduce.5.cloned.1.call-start
  16.6 5.8 copy.20
  22.5 0.0 copy-done.7
  22.5 0.0 copy-start
  22.5 0.0 copy-start.8
  22.5 27.5 %fusion.42 = bf16[448,2304]{1,0:T(8,128)(2,1)} fusion(s32[448,2304]{1,0:T(8,128)} %param.8, s32[14,2304]{1,0:T(8,128)S(1)} %copy-done.7), kind=kLoop, calls=%fused_computation.127 | loop fusion | flops 155860992 | bytes 6322176 | tf_op jit(solution)/shard_map/convert_element_type | solution.py:28
  50.0 0.0 copy-done
  50.0 0.0 copy-done.8
  50.0 0.0 copy-start.9
  50.0 29.5 %fusion.15 = bf16[2304,448]{1,0:T(8,128)(2,1)S(1)} fusion(s32[2304,448]{1,0:T(8,128)S(1)} %copy-done, s32[72,448]{1,0:T(8,128)S(1)} %copy-done.8), kind=kLoop, calls=%fused_computation.94 | loop fusion | flops 155860992 | bytes 6322176 | tf_op jit(solution)/shard_map/convert_element_type | solution.py:28
  79.5 0.0 copy-done.9
  79.5 30.5 %all_gather.3 = bf16[1024,448]{0,1:T(8,128)(2,1)S(1)} all-gather(bf16[128,448]{0,1:T(8,128)(2,1)S(1)} %copy-done.9), channel_id=1, replica_groups=mesh['row'=16,'col'=8,'rep'=2] {'col'}, dimensions={0}, use_global_device_ids=true | all-gather | bytes 1032192 | tf_op jit(solution)/shard_map/all_gather | solution.py:50
  110.1 0.0 copy-start.2
  110.1 0.9 copy-done.2
  111.0 4.3 fusion.10
  115.3 0.0 all-to-all-done
  115.3 6.3 fusion.9
  121.5 0.0 copy-done.6
  121.5 0.0 all-reduce.5.cloned.1.call-update
  121.6 0.0 reduce-scatter.9.cloned.1.call-start
  121.6 415.7 %all-reduce.5.cloned.1.call-done = (bf16[1024,2304]{0,1:T(8,128)(2,1)}, bf16[1024,2304]{0,1:T(8,128)(2,1)}) async-done(((bf16[1024,2304]{0,1:T(8,128)(2,1)}, bf16[1024,2304]{0,1:T(8,128)(2,1)}), (bf16[1024,2304]{0,1:T(8,128)(2,1)}, bf16[1024,2304]{0,1:T(8,128)(2,1)})) %all-reduce.5.cloned.1.call-update) | async-done | bytes 9437200 | tf_op jit(solution)/shard_map/psum | solution.py:57
  537.3 11.3 %fusion.8 = (bf16[1024,2304]{0,1:T(8,128)(2,1)S(1)}, f32[1024,2304]{0,1:T(8,128)}) fusion(bf16[1024,2304]{0,1:T(8,128)(2,1)} %get-tuple-element.4, bf16[1024,2304]{0,1:T(8,128)(2,1)} %get-tuple-element.5), kind=kLoop, calls=%fused_computation.13 | loop fusion | flops 28311552 | bytes 23592960 | tf_op jit(solution)/shard_map/convert_element_type | solution.py:62
  548.7 2.1 copy-done.1
  550.8 0.0 copy-done.4
  550.8 2.3 convolution_convert_fusion.4
  553.1 1.3 copy.25
  554.4 0.0 reduce-scatter.9.cloned.1.call-update
  554.4 0.2 reduce-scatter.7.cloned.1.call-start
  554.7 7.4 convolution_convert_fusion.5
  562.1 1.3 copy.23
  563.4 0.0 reduce-scatter.7.cloned.1.call-update
  563.4 0.0 copy-start.3
  563.4 0.0 all-reduce.7.cloned.1.call-start
  563.5 6.3 fusion.65
  569.8 0.0 copy-done.3
  569.8 8.7 %convolution_convert_fusion.2 = bf16[2304,448]{0,1:T(8,128)(2,1)} fusion(bf16[1024,448]{0,1:T(8,128)(2,1)S(1)} %copy-done.3, f32[1024,2304]{0,1:T(8,128)} %get-tuple-element.9, bf16[1024,2304]{0,1:T(8,128)(2,1)} %get-tuple-element.4), kind=kOutput, calls=%fused_computation.121 | convolution fusion | flops 2122039296 | bytes 17137664 | tf_op jit(solution)/shard_map/dot_general | solution.py:64
  578.5 0.0 all-reduce.7.cloned.1.call-update
  578.5 52.1 %reduce-scatter.9.cloned.1.call-done = bf16[128,448]{1,0:T(8,128)(2,1)} async-done(((bf16[1024,448]{1,0:T(8,128)(2,1)}), bf16[128,448]{1,0:T(8,128)(2,1)}) %reduce-scatter.9.cloned.1.call-update) | async-done | bytes 114704
  630.6 1.7 copy.26
  632.3 78.9 %reduce-scatter.7.cloned.1.call-done = bf16[128,448]{1,0:T(8,128)(2,1)} async-done(((bf16[1024,448]{1,0:T(8,128)(2,1)}), bf16[128,448]{1,0:T(8,128)(2,1)}) %reduce-scatter.7.cloned.1.call-update) | async-done | bytes 114704
  711.2 1.7 copy.24
  712.9 42.6 %all-reduce.7.cloned.1.call-done = (bf16[448,2304]{1,0:T(8,128)(2,1)}, bf16[2304,448]{0,1:T(8,128)(2,1)}) async-done(((bf16[448,2304]{1,0:T(8,128)(2,1)}, bf16[2304,448]{0,1:T(8,128)(2,1)}), (bf16[448,2304]{1,0:T(8,128)(2,1)}, bf16[2304,448]{0,1:T(8,128)(2,1)})) %all-reduce.7.cloned.1.call-update) | async-done | bytes 4128784 | tf_op jit(solution)/shard_map/psum | solution.py:38
  755.5 3.2 copy.40
  758.6 0.0 copy-done.5
  758.6 1.3 copy.41
  (4 shorter events, 0.0 us)
Async XLA Ops:
  9.1 106.2 %all-to-all-start = ((bf16[8,128,448]{1,2,0:T(8,128)(2,1)}), bf16[8,128,448]{1,2,0:T(8,128)(2,1)S(1)}, u32[]{:S(2)}, u32[]{:S(2)}) async-start(bf16[8,128,448]{1,2,0:T(8,128)(2,1)} %stack.2), calls=%async_computation | async-start | bytes 1835008 | tf_op jit(solution)/shard_map/all_to_all | solution.py:48
  16.6 5.9 copy-start.7
  16.6 520.8 %all-reduce.5.cloned.1.call-start = ((), (), s32[]{:S(2)}) async-start(), calls=%async_computation.5 | async-start | bytes 18874368 | tf_op jit(solution)/shard_map/psum | solution.py:57
  22.5 27.5 %copy-start = (s32[2304,448]{1,0:T(8,128)S(1)}, s32[2304,448]{1,0:T(8,128)}, u32[]{:S(2)}) copy-start(s32[2304,448]{1,0:T(8,128)} %copy.20) | copy-start | bytes 12386308
  22.5 27.5 %copy-start.8 = (s32[72,448]{1,0:T(8,128)S(1)}, s32[72,448]{1,0:T(8,128)}, u32[]{:S(2)}) copy-start(s32[72,448]{1,0:T(8,128)} %param.11) | copy-start | bytes 387076
  50.0 29.5 %copy-start.9 = (bf16[128,448]{0,1:T(8,128)(2,1)S(1)}, bf16[128,448]{0,1:T(8,128)(2,1)}, u32[]{:S(2)}) copy-start(bf16[128,448]{0,1:T(8,128)(2,1)} %param.7) | copy-start | bytes 344068
  110.1 0.9 copy-start.2
  115.3 6.3 copy-start.6
  121.6 509.1 %reduce-scatter.9.cloned.1.call-start = ((), (), s32[]{:S(2)}) async-start(), calls=%async_computation.4 | async-start | bytes 1179648
  537.3 13.5 %copy-start.4 = (bf16[448,2304]{1,0:T(8,128)(2,1)S(1)}, bf16[448,2304]{1,0:T(8,128)(2,1)}, u32[]{:S(2)}) copy-start(bf16[448,2304]{1,0:T(8,128)(2,1)} %fusion.42) | copy-start | bytes 6193156
  548.7 2.1 copy-start.1
  554.4 156.8 %reduce-scatter.7.cloned.1.call-start = ((), (), s32[]{:S(2)}) async-start(), calls=%async_computation.3 | async-start | bytes 1179648
  563.4 6.4 copy-start.3
  563.4 192.1 %all-reduce.7.cloned.1.call-start = ((), (), s32[]{:S(2)}) async-start(), calls=%async_computation.6 | async-start | bytes 8257536 | tf_op jit(solution)/shard_map/psum | solution.py:38
  755.5 3.2 copy-start.5
Sparse Core Ops, SparseCore 0:
  121.7 415.6 all-reduce.4
  554.6 76.0 reduce-scatter.8
  635.1 76.0 reduce-scatter.6
  714.5 40.9 all-reduce.6
